TPU v7x, 32 devices: a whole 2x2x4 slice. The times are simulated.
32 devices in a mesh: dp: 16 (over z, y, core), tensor: 2 (over x).
Axes of the slice: x: 2, y: 2, z: 4, core: 2. Of those that a mesh axis runs over, the one named last changes fastest.
Arguments:
- latents_in: bfloat16 [16, 1024, 1152], P('dp', 'tensor'), may hold values from -6 to 6
- steps: int32 [16], P('dp'), may hold values from 0 to 999
- labels: int32 [16], P('dp'), may hold values from 0 to 999
- class_table: bfloat16 [1000, 1152], P(None, 'tensor'), may hold values from -6 to 6
- w_ada: bfloat16 [1152, 6912], P('tensor', 'dp'), may hold values from -0.1875 to 0.1875
- w_qkv: bfloat16 [3, 1152, 1152], P(None, 'dp', 'tensor'), may hold values from -0.1875 to 0.1875
- w_proj: bfloat16 [1152, 1152], P('tensor', 'dp'), may hold values from -3 to 3
- w_fc1: bfloat16 [1152, 4608], P('dp', 'tensor'), may hold values from -0.1875 to 0.1875
- w_fc2: bfloat16 [4608, 1152], P('tensor', 'dp'), may hold values from -0.09375 to 0.09375
- cotangent: bfloat16 [16, 1024, 1152], P('dp', 'tensor'), may hold values from -6 to 6
Outputs:
- block_out: bfloat16 [16, 1024, 1152], P('dp', 'tensor')
- grad_latents: float32 [16, 1024, 1152], P('dp', 'tensor')
- grad_class_table: float32 [1000, 1152], P(None, 'tensor')
- grad_w_ada: float32 [1152, 6912], P('tensor', 'dp')
- grad_w_qkv: float32 [3, 1152, 1152], P(None, 'dp', 'tensor')
- grad_w_proj: float32 [1152, 1152], P('tensor', 'dp')
- grad_w_fc1: float32 [1152, 4608], P('dp', 'tensor')
- grad_w_fc2: float32 [4608, 1152], P('tensor', 'dp')
All inputs are finite; a program needn't handle non-finite values.
Results may differ from a plain program's by a relative error of at most 0.02.
Values may be sent and summed in bfloat16 or wider, within the bound.
A program may use at most 192 MiB of HBM per device.

v0:
```python
import functools
import math
import jax
import jax.numpy as jnp
from jax import lax
from jax.sharding import PartitionSpec as P

D = 1152
H = 16
norm_epsilon = 1e-06
gelu_factor = 0.7978845608028654
gelu_cubic = 0.044715


def norm_rows(rows):
    average = jnp.mean(rows, axis=-1, keepdims=True)
    centred = rows - average
    variance = jnp.mean(centred * centred, axis=-1, keepdims=True)
    inv_std = lax.rsqrt(variance + norm_epsilon)
    return (centred * inv_std, inv_std)


def norm_back(grad_normed, normed, inv_std):
    first = jnp.mean(grad_normed, axis=-1, keepdims=True)
    second = jnp.mean(grad_normed * normed, axis=-1, keepdims=True)
    return inv_std * (grad_normed - first - normed * second)


def gelu_value(pre):
    inner = gelu_factor * (pre + gelu_cubic * pre * pre * pre)
    return 0.5 * pre * (1.0 + jnp.tanh(inner))


def gelu_slope(pre):
    tangent = jnp.tanh(gelu_factor * (pre + gelu_cubic * pre * pre * pre))
    return 0.5 * (1.0 + tangent) + 0.5 * pre * (1.0 - tangent * tangent) * gelu_factor * (
        1.0 + 3.0 * gelu_cubic * pre * pre
    )


def silu_value(value):
    return value * jax.nn.sigmoid(value)


def silu_slope(value):
    sigma = jax.nn.sigmoid(value)
    return sigma * (1.0 + value * (1.0 - sigma))


def time_columns(steps_float, columns, width):
    half = width // 2
    index = jnp.where(columns < half, columns, columns - half).astype(jnp.float32)
    freqs = jnp.exp(-math.log(10000.0) * index / half)
    angles = steps_float[:, None] * freqs[None, :]
    return jnp.where(columns[None, :] < half, jnp.cos(angles), jnp.sin(angles))


def attend(queries, keys, values, score_scale):
    scores = (
        jnp.einsum("qhd,khd->hqk", queries, keys, preferred_element_type=jnp.float32) * score_scale
    )
    largest = jnp.max(scores, axis=-1, keepdims=True)
    log_total = largest + jnp.log(jnp.sum(jnp.exp(scores - largest), axis=-1, keepdims=True))
    probs = jnp.exp(scores - log_total).astype(jnp.bfloat16)
    mixed = jnp.einsum("hqk,khd->qhd", probs, values, preferred_element_type=jnp.float32)
    return (mixed.astype(jnp.bfloat16), log_total[:, :, 0])


def attend_back(queries, keys, values, mixed, grad_mixed, log_totals, score_scale):
    scores = (
        jnp.einsum("qhd,khd->hqk", queries, keys, preferred_element_type=jnp.float32) * score_scale
    )
    probs = jnp.exp(scores - log_totals[:, :, None])
    grad_values = jnp.einsum(
        "hqk,qhd->khd", probs.astype(jnp.bfloat16), grad_mixed, preferred_element_type=jnp.float32
    )
    grad_probs = jnp.einsum("qhd,khd->hqk", grad_mixed, values, preferred_element_type=jnp.float32)
    delta = jnp.sum(grad_mixed.astype(jnp.float32) * mixed.astype(jnp.float32), axis=-1)
    grad_scores = (
        probs * (grad_probs - jnp.swapaxes(delta, 0, 1)[:, :, None]) * score_scale
    ).astype(jnp.bfloat16)
    grad_queries = jnp.einsum("hqk,khd->qhd", grad_scores, keys, preferred_element_type=jnp.float32)
    grad_keys = jnp.einsum("hqk,qhd->khd", grad_scores, queries, preferred_element_type=jnp.float32)
    return (grad_queries, grad_keys, grad_values)


def from_rank(value, ranks, step):
    return lax.ppermute(value, "tensor", [(i, (i - step) % ranks) for i in range(ranks)])


def fetch_rest(rows, ranks):
    got = [from_rank(rows, ranks, step) for step in range(1, ranks)]
    return got[0] if ranks == 2 else jnp.concatenate(got, axis=0)


def return_rest(partial, ranks):
    size = partial.shape[0] // (ranks - 1)
    total = None
    for step in range(1, ranks):
        part = partial[(step - 1) * size : step * size].astype(jnp.bfloat16)
        part = from_rank(part, ranks, ranks - step).astype(jnp.float32)
        total = part if total is None else total + part
    return total


def sum_ranks(value, ranks):
    total = value
    for step in range(1, ranks):
        total = total + from_rank(value, ranks, step)
    return total


def dot(spec, left, right):
    return jnp.einsum(spec, left, right, preferred_element_type=jnp.float32)


def join(own, rest):
    return jnp.concatenate([own, rest], axis=0)


def shards(
    ranks, latents_in, steps, labels, class_table, w_ada, w_qkv, w_proj, w_fc1, w_fc2, cotangent
):
    half = jnp.bfloat16
    rank = lax.axis_index("tensor")
    width = latents_in.shape[2]
    mine = latents_in.shape[1]
    owned = class_table.shape[1]
    head_size = D // H
    heads_here = owned // head_size
    score_scale = head_size ** (-0.5)
    highest = lax.Precision.HIGHEST
    marks = lax.all_gather(jnp.stack([steps, labels], axis=1), "dp", axis=0, tiled=True)
    all_steps, all_labels = (marks[:, 0], marks[:, 1])
    attn_w = lax.all_gather(
        jnp.concatenate([w_qkv[0], w_qkv[1], w_qkv[2], w_proj.T], axis=1), "dp", axis=0, tiled=True
    )
    mlp_w = lax.all_gather(jnp.concatenate([w_fc1, w_fc2.T], axis=1), "dp", axis=0, tiled=True)
    qkv_full, proj_t = (attn_w[:, : 3 * owned], attn_w[:, 3 * owned :])
    fc1_full, fc2_t = (mlp_w[:, : w_fc1.shape[1]], mlp_w[:, w_fc1.shape[1] :])
    columns = rank * owned + jnp.arange(owned, dtype=jnp.int32)
    classes = jnp.arange(class_table.shape[0], dtype=jnp.int32)
    one_hot = (all_labels[:, None] == classes[None, :]).astype(half)
    cond = time_columns(all_steps.astype(jnp.float32), columns, D) + jnp.dot(
        one_hot, class_table, preferred_element_type=jnp.float32
    )
    cond_half = silu_value(cond).astype(half)
    mod_part = jnp.dot(cond_half, w_ada, preferred_element_type=jnp.float32)
    modulation = lax.all_to_all(sum_ranks(mod_part, ranks), "dp", 0, 0, tiled=True)
    modulation = modulation.reshape(6, width)
    shift_a, scale_a, gate_a = (modulation[0], modulation[1], modulation[2])
    shift_m, scale_m, gate_m = (modulation[3], modulation[4], modulation[5])
    rows_in = latents_in[0].astype(jnp.float32)
    normed_a, inv_a = norm_rows(rows_in)
    mod_a = (normed_a * (1.0 + scale_a) + shift_a).astype(half)
    rest_a = fetch_rest(mod_a, ranks)
    grad_out = cotangent[0].astype(jnp.float32)
    grad_mlp = (grad_out * gate_m).astype(half)
    rest_grad_m = fetch_rest(grad_mlp, ranks)
    qkv_own = dot("td,dc->tc", mod_a, qkv_full).astype(half)
    qkv_rest = dot("td,dc->tc", rest_a, qkv_full).astype(half)
    projected = join(qkv_own, qkv_rest)
    tokens = projected.shape[0]
    queries = projected[:, :owned].reshape(tokens, heads_here, head_size)
    keys = projected[:, owned : 2 * owned].reshape(tokens, heads_here, head_size)
    values = projected[:, 2 * owned :].reshape(tokens, heads_here, head_size)
    mixed_rest, log_rest = attend(queries[mine:], keys, values, score_scale)
    mixed_rest_flat = mixed_rest.reshape(tokens - mine, owned)
    attn_away = return_rest(dot("tc,dc->td", mixed_rest_flat, proj_t), ranks)
    mixed_own, log_own = attend(queries[:mine], keys, values, score_scale)
    mixed_own_flat = mixed_own.reshape(mine, owned)
    attn_out = dot("tc,dc->td", mixed_own_flat, proj_t) + attn_away
    hidden = rows_in + gate_a * attn_out
    normed_m, inv_m = norm_rows(hidden)
    mod_m = (normed_m * (1.0 + scale_m) + shift_m).astype(half)
    rest_m = fetch_rest(mod_m, ranks)
    pre_own = dot("td,df->tf", mod_m, fc1_full)
    acts_own = gelu_value(pre_own).astype(half)
    pre_rest = dot("td,df->tf", rest_m, fc1_full)
    acts_rest = gelu_value(pre_rest).astype(half)
    mlp_away = return_rest(dot("tf,df->td", acts_rest, fc2_t), ranks)
    grad_pre_rest = (dot("td,df->tf", rest_grad_m, fc2_t) * gelu_slope(pre_rest)).astype(half)
    grad_mod_away = return_rest(dot("tf,df->td", grad_pre_rest, fc1_full), ranks)
    mlp_out = dot("tf,df->td", acts_own, fc2_t) + mlp_away
    block_out = (hidden + gate_m * mlp_out).astype(half)
    grad_gate_m = jnp.sum(grad_out * mlp_out, axis=0)
    grad_pre_own = (dot("td,df->tf", grad_mlp, fc2_t) * gelu_slope(pre_own)).astype(half)
    grad_mod_m = dot("tf,df->td", grad_pre_own, fc1_full) + grad_mod_away
    grad_fc2_t = dot("td,tf->df", join(grad_mlp, rest_grad_m), join(acts_own, acts_rest))
    grad_fc1 = dot("td,tf->df", join(mod_m, rest_m), join(grad_pre_own, grad_pre_rest))
    mlp_w_part = jnp.concatenate([grad_fc1.astype(half), grad_fc2_t.astype(half)], axis=1)
    mlp_w_part, grad_mod_m = lax.optimization_barrier((mlp_w_part, grad_mod_m))
    grad_mlp_w = lax.psum_scatter(mlp_w_part, "dp", scatter_dimension=0, tiled=True).astype(
        jnp.float32
    )
    grad_shift_m = jnp.sum(grad_mod_m, axis=0)
    grad_scale_m = jnp.sum(grad_mod_m * normed_m, axis=0)
    grad_hidden = grad_out + norm_back(grad_mod_m * (1.0 + scale_m), normed_m, inv_m)
    grad_gate_a = jnp.sum(grad_hidden * attn_out, axis=0)
    grad_attn = (grad_hidden * gate_a).astype(half)
    rest_grad_a = fetch_rest(grad_attn, ranks)
    grad_mixed_own = dot("td,dc->tc", grad_attn, proj_t).astype(half)
    grad_mixed_rest = dot("td,dc->tc", rest_grad_a, proj_t).astype(half)
    mixed_flat = join(mixed_own_flat, mixed_rest_flat)
    grad_proj_t = dot("td,tc->dc", join(grad_attn, rest_grad_a), mixed_flat)
    grad_mixed = join(grad_mixed_own, grad_mixed_rest)
    grads = attend_back(
        queries,
        keys,
        values,
        mixed_flat.reshape(tokens, heads_here, head_size),
        grad_mixed.reshape(tokens, heads_here, head_size),
        jnp.concatenate([log_own, log_rest], axis=1),
        score_scale,
    )
    grad_qkv = jnp.concatenate([g.astype(half).reshape(tokens, owned) for g in grads], axis=1)
    grad_a_away = return_rest(dot("tc,dc->td", grad_qkv[mine:], qkv_full), ranks)
    grad_w_qkv = dot("td,tc->dc", join(mod_a, rest_a), grad_qkv)
    attn_w_part = jnp.concatenate([grad_w_qkv.astype(half), grad_proj_t.astype(half)], axis=1)
    attn_w_part, grad_mlp_w = lax.optimization_barrier((attn_w_part, grad_mlp_w))
    grad_attn_w = lax.psum_scatter(attn_w_part, "dp", scatter_dimension=0, tiled=True).astype(
        jnp.float32
    )
    grad_mod_a = dot("tc,dc->td", grad_qkv[:mine], qkv_full) + grad_a_away
    grad_shift_a = jnp.sum(grad_mod_a, axis=0)
    grad_scale_a = jnp.sum(grad_mod_a * normed_a, axis=0)
    grad_input = grad_hidden + norm_back(grad_mod_a * (1.0 + scale_a), normed_a, inv_a)
    grad_mod_part = jnp.stack(
        [grad_shift_a, grad_scale_a, grad_gate_a, grad_shift_m, grad_scale_m, grad_gate_m]
    ).reshape(all_steps.shape[0], w_ada.shape[1])
    grad_modulation = lax.all_to_all(sum_ranks(grad_mod_part, ranks), "dp", 0, 0, tiled=True)
    grad_ada = jnp.einsum(
        "lc,lm->cm", cond_half.astype(jnp.float32), grad_modulation, precision=highest
    )
    grad_cond = lax.psum(
        jnp.einsum("lm,cm->lc", grad_modulation, w_ada.astype(jnp.float32), precision=highest), "dp"
    ) * silu_slope(cond)
    grad_table = jnp.einsum("ln,lc->nc", one_hot.astype(jnp.float32), grad_cond, precision=highest)
    return (
        block_out[None],
        grad_input[None],
        grad_table,
        grad_ada,
        jnp.stack([grad_attn_w[:, j * owned : (j + 1) * owned] for j in range(3)]),
        grad_attn_w[:, 3 * owned :].T,
        grad_mlp_w[:, : w_fc1.shape[1]],
        grad_mlp_w[:, w_fc1.shape[1] :].T,
    )


def solution(mesh):
    return jax.shard_map(
        functools.partial(shards, mesh.shape["tensor"]),
        mesh=mesh,
        in_specs=(
            P("dp", "tensor", None),
            P("dp"),
            P("dp"),
            P(None, "tensor"),
            P("tensor", "dp"),
            P(None, "dp", "tensor"),
            P("tensor", "dp"),
            P("dp", "tensor"),
            P("tensor", "dp"),
            P("dp", "tensor", None),
        ),
        out_specs=(
            P("dp", "tensor", None),
            P("dp", "tensor", None),
            P(None, "tensor"),
            P("tensor", "dp"),
            P(None, "dp", "tensor"),
            P("tensor", "dp"),
            P("dp", "tensor"),
            P("tensor", "dp"),
        ),
        check_vma=False,
    )
```

profile of v0, /device:TPU:0, one launch (start us, length us, event | category | flops | bytes accessed | tf_op | source)
XLA Modules:
  0.0 526.4 jit_solution(4783316110772384095)
XLA Ops:
  13.7 23.3 %all-gather = s32[16,1,2]{2,1,0:T(1,128)S(1)} all-gather(s32[1,1,2]{2,1,0:T(1,128)S(1)} %add_bitcast_fusion.1), channel_id=1, replica_groups=mesh['dp'=16,'tensor'=2] {'dp'}, dimensions={0}, use_global_device_ids=true | all-gather | bytes 136 | tf_op jit(solution)/shard_map/all_gather | solution.py:133
  46.3 7.2 %all-to-all-done = f32[16,1,432]{2,1,0:T(1,128)S(1)} async-done(((f32[16,1,432]{2,1,0:T(1,128)}), f32[16,1,432]{2,1,0:T(1,128)S(1)}, u32[]{:S(2)}, u32[]{:S(2)}) %all-to-all-start) | async-done | bytes 27680 | tf_op jit(solution)/shard_map/all_to_all | solution.py:149
  56.5 25.9 %collective-permute-done.1 = bf16[512,1152]{1,0:T(8,128)(2,1)S(1)} collective-permute-done((bf16[512,1152]{1,0:T(8,128)(2,1)S(1)}, bf16[512,1152]{1,0:T(8,128)(2,1)S(1)}, u32[]{:S(2)}, u32[]{:S(2)}) %collective-permute-start.1) | collective-permute-done | bytes 1179680 | tf_op jit(solution)/shard_map/ppermute | solution.py:88
  118.2 14.8 %collective-permute-done.2 = bf16[512,1152]{1,0:T(8,128)(2,1)S(1)} collective-permute-done((bf16[512,1152]{1,0:T(8,128)(2,1)S(1)}, bf16[512,1152]{1,0:T(8,128)(2,1)S(1)}, u32[]{:S(2)}, u32[]{:S(2)}) %collective-permute-start.2) | collective-permute-done | bytes 1179680 | tf_op jit(solution)/shard_map/ppermute | solution.py:88
  142.5 25.7 %collective-permute-done.3 = bf16[512,1152]{1,0:T(8,128)(2,1)} collective-permute-done((bf16[512,1152]{1,0:T(8,128)(2,1)S(1)}, bf16[512,1152]{1,0:T(8,128)(2,1)}, u32[]{:S(2)}, u32[]{:S(2)}) %collective-permute-start.3) | collective-permute-done | bytes 1179680 | tf_op jit(solution)/shard_map/ppermute | solution.py:88
  168.1 8.4 %multiply_convert_fusion.1 = (bf16[512,2304]{1,0:T(8,128)(2,1)}, f32[512,2304]{1,0:T(8,128)S(1)}) fusion(bf16[512,1152]{1,0:T(8,128)(2,1)} %collective-permute-done.3, bf16[1152,4608]{1,0:T(8,128)(2,1)} %all-gather.6.cloned.1.call-done), kind=kOutput, calls=%fused_computation.39 | convolution fusion | flops 2728525824 | bytes 13565952 | tf_op jit(solution)/shard_map/td,df->tf/dot_general | solution.py:114
  176.5 13.8 %collective-permute-done.5 = bf16[512,1152]{1,0:T(8,128)(2,1)} collective-permute-done((bf16[512,1152]{1,0:T(8,128)(2,1)}, bf16[512,1152]{1,0:T(8,128)(2,1)}, u32[]{:S(2)}, u32[]{:S(2)}) %collective-permute-start.5) | collective-permute-done | bytes 1179680 | tf_op jit(solution)/shard_map/ppermute | solution.py:88
  206.6 7.4 %fusion.21 = bf16[512,2304]{1,0:T(8,128)(2,1)S(1)} fusion(f32[512,2304]{1,0:T(8,128)S(1)} %get-tuple-element.74, bf16[512,1152]{1,0:T(8,128)(2,1)} %fusion.65, bf16[1152,4608]{1,0:T(8,128)(2,1)S(1)} %copy-done.56), kind=kOutput, calls=%fused_computation.41 | convolution fusion | flops 2740322304 | bytes 13565952 | tf_op jit(solution)/shard_map/td,df->tf/dot_general | solution.py:114
  214.0 9.1 %convolution_convert_fusion.1 = bf16[1152,2304]{1,0:T(8,128)(2,1)S(1)} fusion(bf16[512,2304]{1,0:T(8,128)(2,1)} %copy-done.62, bf16[512,2304]{1,0:T(8,128)(2,1)S(1)} %fusion.21, bf16[512,1152]{1,0:T(8,128)(2,1)} %collective-permute-done.3, bf16[512,1152]{1,0:T(8,128)(2,1)S(1)} %copy-done.28), kind=kOutput, calls=%fused_computation.11 | convolution fusion | flops 5452627968 | bytes 12386304 | tf_op jit(solution)/shard_map/td,tf->df/dot_general | solution.py:114
  223.2 7.9 %convolution_convert_fusion = bf16[1152,2304]{1,0:T(8,128)(2,1)S(1)} fusion(bf16[512,2304]{1,0:T(8,128)(2,1)S(1)} %copy-done.61, bf16[512,2304]{1,0:T(8,128)(2,1)S(1)} %get-tuple-element.73, bf16[512,1152]{1,0:T(8,128)(2,1)} %collective-permute-done.5, bf16[512,1152]{1,0:T(8,128)(2,1)} %fusion.65), kind=kOutput, calls=%fused_computation.10 | convolution fusion | flops 5452627968 | bytes 12386304 | tf_op jit(solution)/shard_map/td,tf->df/dot_general | solution.py:114
  235.6 8.2 %convert_add_fusion.2 = f32[512,1152]{1,0:T(8,128)} fusion(bf16[512,1152]{1,0:T(8,128)(2,1)} %collective-permute-done.6, bf16[512,2304]{1,0:T(8,128)(2,1)} %copy-done.58, bf16[1152,4608]{1,0:T(8,128)(2,1)} %all-gather.6.cloned.1.call-done), kind=kOutput, calls=%fused_computation.116 | convolution fusion | flops 2719088640 | bytes 11206656 | tf_op jit(solution)/shard_map/tf,df->td/dot_general | solution.py:114
  251.9 6.8 %fusion.27 = f32[512,1152]{1,0:T(8,128)S(1)} fusion(bf16[512,2304]{1,0:T(8,128)(2,1)S(1)} %copy-done.60, bf16[1152,4608]{1,0:T(8,128)(2,1)} %all-gather.6.cloned.1.call-done), kind=kOutput, calls=%fused_computation.55 | convolution fusion | flops 2717908992 | bytes 10027008 | tf_op jit(solution)/shard_map/tf,df->td/dot_general | solution.py:114
  260.3 15.6 %collective-permute-done.4 = bf16[512,1152]{1,0:T(8,128)(2,1)S(1)} collective-permute-done((bf16[512,1152]{1,0:T(8,128)(2,1)S(1)}, bf16[512,1152]{1,0:T(8,128)(2,1)S(1)}, u32[]{:S(2)}, u32[]{:S(2)}) %collective-permute-start.4) | collective-permute-done | bytes 1179680 | tf_op jit(solution)/shard_map/ppermute | solution.py:88
  282.2 13.3 %fusion.134 = f32[8,1024,1024]{2,1,0:T(8,128)} fusion(bf16[1024,8,72]{0,2,1:T(8,128)(2,1)S(1)} %bitcast.145, bf16[1024,8,72]{0,2,1:T(8,128)(2,1)S(1)} %bitcast.140), kind=kOutput, calls=%fused_computation.218 | convolution fusion | flops 1207959552 | bytes 35913728 | tf_op jit(solution)/shard_map/qhd,khd->hqk/dot_general | solution.py:71
  297.1 8.3 %collective-permute-done.7 = bf16[512,1152]{1,0:T(8,128)(2,1)S(1)} collective-permute-done((bf16[512,1152]{1,0:T(8,128)(2,1)S(1)}, bf16[512,1152]{1,0:T(8,128)(2,1)S(1)}, u32[]{:S(2)}, u32[]{:S(2)}) %collective-permute-start.7) | collective-permute-done | bytes 1179680 | tf_op jit(solution)/shard_map/ppermute | solution.py:88
  310.3 19.7 %multiply_convert_fusion = bf16[8,1024,1024]{2,1,0:T(8,128)(2,1)} fusion(f32[8,1024,1024]{2,1,0:T(8,128)} %fusion.134, f32[8,1024]{1,0:T(8,128)S(1)} %bitcast.170, f32[8,1024]{1,0:T(8,128)S(1)} %pad_maximum_fusion.7, bf16[1024,8,72]{0,2,1:T(8,128)(2,1)S(1)} %bitcast.143, bf16[1024,8,72]{0,2,1:T(8,128)(2,1)S(1)} %bitcast.149), kind=kOutput, calls=%fused_computation | convolution fusion | flops 1258291200 | bytes 52756480 | tf_op jit(solution)/shard_map/qhd,khd->hqk/dot_general | solution.py:77
  330.0 9.1 %convolution_convert_fusion.8 = bf16[8,72,1024]{2,1,0:T(8,128)(2,1)S(1)} fusion(bf16[1024,8,72]{0,2,1:T(8,128)(2,1)S(1)} %bitcast.146, bf16[8,1024,1024]{2,1,0:T(8,128)(2,1)} %multiply_convert_fusion), kind=kOutput, calls=%fused_computation.128 | convolution fusion | flops 1208549376 | bytes 19136512 | tf_op jit(solution)/shard_map/hqk,qhd->khd/dot_general | solution.py:83
  339.1 12.1 %convolution_convert_fusion.9 = bf16[8,72,1024]{2,1,0:T(8,128)(2,1)} fusion(bf16[1024,8,72]{0,2,1:T(8,128)(2,1)S(1)} %bitcast.141, bf16[8,1024,1024]{2,1,0:T(8,128)(2,1)} %multiply_convert_fusion), kind=kOutput, calls=%fused_computation.129 | convolution fusion | flops 1208549376 | bytes 19136512 | tf_op jit(solution)/shard_map/hqk,khd->qhd/dot_general | solution.py:82
  351.2 13.2 %fusion.85 = bf16[8,72,1024]{2,1,0:T(8,128)(2,1)S(1)} fusion(bf16[1024,8,72]{0,2,1:T(8,128)(2,1)S(1)} %bitcast.144, f32[8,1024,1024]{2,1,0:T(8,128)} %fusion.134, f32[8,1024]{1,0:T(8,128)} %copy-done.29), kind=kOutput, calls=%fused_computation.127 | convolution fusion | flops 1233715200 | bytes 35946496 | tf_op jit(solution)/shard_map/hqk,qhd->khd/dot_general | solution.py:74
  364.4 9.1 %convolution_convert_fusion.2 = bf16[1152,1728]{0,1:T(8,128)(2,1)S(1)} fusion(bf16[512,1152]{1,0:T(8,128)(2,1)} %copy-done.57, bf16[512,1152]{1,0:T(8,128)(2,1)} %copy-done.26, bf16[1024,576]{0,1:T(8,128)(2,1)S(1)} %bitcast.150, bf16[1024,576]{0,1:T(8,128)(2,1)S(1)} %bitcast.155, bf16[1024,576]{0,1:T(8,128)(2,1)S(1)} %bitcast.157), kind=kOutput, calls=%fused_computation.15 | convolution fusion | flops 4094189568 | bytes 9879552 | tf_op jit(solution)/shard_map/td,tc->dc/dot_general | solution.py:114
  378.6 8.6 %copy.25 = bf16[1152,2304]{1,0:T(8,128)(2,1)} copy(bf16[1152,2304]{0,1:T(8,128)(2,1)} %pad_maximum_fusion.1) | data formatting | bytes 10616832
  398.0 19.8 %collective-permute-done.8 = bf16[512,1152]{1,0:T(8,128)(2,1)S(1)} collective-permute-done((bf16[512,1152]{1,0:T(8,128)(2,1)S(1)}, bf16[512,1152]{1,0:T(8,128)(2,1)S(1)}, u32[]{:S(2)}, u32[]{:S(2)}) %collective-permute-start.8) | collective-permute-done | bytes 1179680 | tf_op jit(solution)/shard_map/ppermute | solution.py:88
  432.7 8.6 %all-to-all-start.1 = ((f32[16,1,432]{2,1,0:T(1,128)}), f32[16,1,432]{2,1,0:T(1,128)}, u32[]{:S(2)}, u32[]{:S(2)}) async-start(f32[16,1,432]{2,1,0:T(1,128)} %all_to_all.16), calls=%async_computation.1 | async-start | bytes 65536 | tf_op jit(solution)/shard_map/all_to_all | solution.py:231
  449.4 59.8 %psum.7 = f32[16,576]{1,0:T(8,128)S(1)} all-reduce(f32[16,576]{1,0:T(8,128)S(1)} %fusion.110), channel_id=1, replica_groups=mesh['dp'=16,'tensor'=2] {'dp'}, use_global_device_ids=true, to_apply=%region_19.20 | all-reduce | flops 9216 | bytes 73728 | tf_op jit(solution)/shard_map/psum | solution.py:235
  (247 shorter events, 154.7 us)
Async XLA Ops:
  7.2 75.1 %all-gather.4.cloned.1.call-start = ((), (), s32[]{:S(2)}) async-start(), calls=%async_computation.4 | async-start | bytes 5640192 | tf_op jit(solution)/shard_map/all_gather | solution.py:135
  10.3 157.8 %all-gather.6.cloned.1.call-start = ((), (), s32[]{:S(2)}) async-start(), calls=%async_computation.5 | async-start | bytes 11280384 | tf_op jit(solution)/shard_map/all_gather | solution.py:138
  38.2 3.9 collective-permute-start
  39.9 47.6 %copy-start.49 = (f32[512]{0:T(512)}, f32[512]{0:T(512)S(1)}, u32[]{:S(2)}) copy-start(f32[512]{0:T(512)S(1)} %broadcast_multiply_fusion.5) | copy-start | bytes 6148
  42.8 10.7 %all-to-all-start = ((f32[16,1,432]{2,1,0:T(1,128)}), f32[16,1,432]{2,1,0:T(1,128)S(1)}, u32[]{:S(2)}, u32[]{:S(2)}) async-start(f32[16,1,432]{2,1,0:T(1,128)} %copy.22), calls=%async_computation | async-start | bytes 65536 | tf_op jit(solution)/shard_map/all_to_all | solution.py:149
  46.3 330.1 %reduce-scatter.5.cloned.1.call-start = ((), (), s32[]{:S(2)}) async-start(), calls=%async_computation.6 | async-start | bytes 11280384 | tf_op jit(solution)/shard_map/reduce_scatter | solution.py:193
  46.3 41.2 %copy-start.52 = (f32[512]{0:T(512)}, f32[512]{0:T(512)S(1)}, u32[]{:S(2)}) copy-start(f32[512]{0:T(512)S(1)} %add_rsqrt_fusion.1) | copy-start | bytes 6148
  54.9 32.6 %copy-start.26 = (bf16[512,1152]{1,0:T(8,128)(2,1)}, bf16[512,1152]{1,0:T(8,128)(2,1)S(1)}, u32[]{:S(2)}) copy-start(bf16[512,1152]{1,0:T(8,128)(2,1)S(1)} %fusion.57) | copy-start | bytes 3538948
  55.0 27.4 %collective-permute-start.1 = (bf16[512,1152]{1,0:T(8,128)(2,1)S(1)}, bf16[512,1152]{1,0:T(8,128)(2,1)S(1)}, u32[]{:S(2)}, u32[]{:S(2)}) collective-permute-start(bf16[512,1152]{1,0:T(8,128)(2,1)S(1)} %fusion.57), channel_id=1, source_target_pairs={{0,1},{1,0},{2,3},{3,2},{4,5},{5,4},{6,7},{7,6},{8,9},{9,8},{10,11... | collective-permute-start | bytes 3538952 | tf_op jit(solution)/shard_map/ppermute | solution.py:88
  106.4 26.6 %collective-permute-start.2 = (bf16[512,1152]{1,0:T(8,128)(2,1)S(1)}, bf16[512,1152]{1,0:T(8,128)(2,1)S(1)}, u32[]{:S(2)}, u32[]{:S(2)}) collective-permute-start(bf16[512,1152]{1,0:T(8,128)(2,1)S(1)} %convolution_convert_fusion.5), channel_id=1, source_target_pairs={{0,1},{1,0},{2,3},{3,2},{4,5},{5,4},{6,7},{7,6},{8,9},{9,8},{10,11... | collective-permute-start | bytes 3538952 | tf_op jit(solution)/shard_map/ppermute | solution.py:88
  139.1 29.0 %collective-permute-start.3 = (bf16[512,1152]{1,0:T(8,128)(2,1)S(1)}, bf16[512,1152]{1,0:T(8,128)(2,1)}, u32[]{:S(2)}, u32[]{:S(2)}) collective-permute-start(bf16[512,1152]{1,0:T(8,128)(2,1)S(1)} %add_convert_fusion.1), channel_id=1, source_target_pairs={{0,1},{1,0},{2,3},{3,2},{4,5},{5,4},{6,7},{7,6},{8,9},{9,8},{10,11... | collective-permute-start | bytes 3538952 | tf_op jit(solution)/shard_map/ppermute | solution.py:88
  141.9 48.4 %collective-permute-start.5 = (bf16[512,1152]{1,0:T(8,128)(2,1)}, bf16[512,1152]{1,0:T(8,128)(2,1)}, u32[]{:S(2)}, u32[]{:S(2)}) collective-permute-start(bf16[512,1152]{1,0:T(8,128)(2,1)} %fusion.65), channel_id=1, source_target_pairs={{0,1},{1,0},{2,3},{3,2},{4,5},{5,4},{6,7},{7,6},{8,9},{9,8},{10,11... | collective-permute-start | bytes 3538952 | tf_op jit(solution)/shard_map/ppermute | solution.py:88
  201.2 34.4 %collective-permute-start.6 = (bf16[512,1152]{1,0:T(8,128)(2,1)}, bf16[512,1152]{1,0:T(8,128)(2,1)}, u32[]{:S(2)}, u32[]{:S(2)}) collective-permute-start(bf16[512,1152]{1,0:T(8,128)(2,1)} %fusion.37), channel_id=1, source_target_pairs={{0,1},{1,0},{2,3},{3,2},{4,5},{5,4},{6,7},{7,6},{8,9},{9,8},{10,11... | collective-permute-start | bytes 3538952 | tf_op jit(solution)/shard_map/ppermute | solution.py:88
  243.8 272.4 %reduce-scatter.7.cloned.1.call-start = ((), (), s32[]{:S(2)}) async-start(), calls=%async_computation.7 | async-start | bytes 5640192
  244.6 65.7 %copy-start.29 = (f32[8,1024]{1,0:T(8,128)}, f32[8,1024]{1,0:T(8,128)S(1)}, u32[]{:S(2)}) copy-start(f32[8,1024]{1,0:T(8,128)S(1)} %pad_maximum_fusion.7) | copy-start | bytes 98308
  251.2 24.7 %collective-permute-start.4 = (bf16[512,1152]{1,0:T(8,128)(2,1)S(1)}, bf16[512,1152]{1,0:T(8,128)(2,1)S(1)}, u32[]{:S(2)}, u32[]{:S(2)}) collective-permute-start(bf16[512,1152]{1,0:T(8,128)(2,1)S(1)} %fusion.40), channel_id=1, source_target_pairs={{0,1},{1,0},{2,3},{3,2},{4,5},{5,4},{6,7},{7,6},{8,9},{9,8},{10,11... | collective-permute-start | bytes 3538952 | tf_op jit(solution)/shard_map/ppermute | solution.py:88
  281.6 23.8 %collective-permute-start.7 = (bf16[512,1152]{1,0:T(8,128)(2,1)S(1)}, bf16[512,1152]{1,0:T(8,128)(2,1)S(1)}, u32[]{:S(2)}, u32[]{:S(2)}) collective-permute-start(bf16[512,1152]{1,0:T(8,128)(2,1)S(1)} %multiply_convert_fusion.3), channel_id=1, source_target_pairs={{0,1},{1,0},{2,3},{3,2},{4,5},{5,4},{6,7},{7,6},{8,9},{9,8},{10,11... | collective-permute-start | bytes 3538952 | tf_op jit(solution)/shard_map/ppermute | solution.py:88
  394.3 23.4 %collective-permute-start.8 = (bf16[512,1152]{1,0:T(8,128)(2,1)S(1)}, bf16[512,1152]{1,0:T(8,128)(2,1)S(1)}, u32[]{:S(2)}, u32[]{:S(2)}) collective-permute-start(bf16[512,1152]{1,0:T(8,128)(2,1)S(1)} %convolution_convert_fusion.4), channel_id=1, source_target_pairs={{0,1},{1,0},{2,3},{3,2},{4,5},{5,4},{6,7},{7,6},{8,9},{9,8},{10,11... | collective-permute-start | bytes 3538952 | tf_op jit(solution)/shard_map/ppermute | solution.py:88
  397.9 43.4 %copy-start.6 = (f32[512,1152]{1,0:T(8,128)S(1)}, f32[512,1152]{1,0:T(8,128)}, u32[]{:S(2)}) copy-start(f32[512,1152]{1,0:T(8,128)} %copy-done.5) | copy-start | bytes 7077892
  398.0 43.4 %copy-start.51 = (f32[512]{0:T(512)S(1)}, f32[512]{0:T(512)}, u32[]{:S(2)}) copy-start(f32[512]{0:T(512)} %copy-done.49) | copy-start | bytes 6148
  398.0 43.4 %copy-start.54 = (f32[512]{0:T(512)S(1)}, f32[512]{0:T(512)}, u32[]{:S(2)}) copy-start(f32[512]{0:T(512)} %copy-done.52) | copy-start | bytes 6148
  427.2 4.1 collective-permute-start.9
  432.7 15.3 %all-to-all-start.1 = ((f32[16,1,432]{2,1,0:T(1,128)}), f32[16,1,432]{2,1,0:T(1,128)}, u32[]{:S(2)}, u32[]{:S(2)}) async-start(f32[16,1,432]{2,1,0:T(1,128)} %all_to_all.16), calls=%async_computation.1 | async-start | bytes 65536 | tf_op jit(solution)/shard_map/all_to_all | solution.py:231
  445.2 69.8 %copy-start.12 = (f32[72,4608]{1,0:T(8,128)S(1)}, f32[72,4608]{1,0:T(8,128)}, u32[]{:S(2)}) copy-start(f32[72,4608]{1,0:T(8,128)} %convert_element_type.207) | copy-start | bytes 3981316
  (60 other events, 678.0 us)
Sparse Core Ops, SparseCore 0:
  10.7 59.4 all-gather.3
  73.0 86.9 all-gather.5
  243.9 120.1 reduce-scatter.4
  387.3 80.5 reduce-scatter.6
where the time goes:
time: 534 us; the launch traced here: 526 us
  matrix products  198 us (37%)
  waiting for transfers between devices  137 us (26%)
  blocking collectives  83.1 us (16%)
  other arithmetic  41.1 us (8%)
  local copies, waits for them, and re-layouts  27.7 us (5%)
  starting transfers between devices  23.1 us (4%)
  between operations  16.3 us (3%)
    ppermute x10, waiting for transfers between devices, from_rank(): lax.ppermute(value, 'tensor', [(i, (i - step) % ranks) for i in range(ran...  127 us
    dot_general x20, matrix products, dot(): return jnp.einsum(spec, left, right, preferred_element_type=jnp.float32)  110 us
    psum x1, blocking collectives, shards(): lax.psum(jnp.einsum('lm,cm->lc', grad_modulation, w_ada.astype(jnp.float3...  59.8 us
    all_gather x1, blocking collectives, shards(): lax.all_gather(jnp.stack([steps, labels], axis=1), 'dp', axis=0, tiled=True)  23.3 us
    dot_general x1, matrix products, attend_back(): jnp.einsum('qhd,khd->hqk', grad_mixed, values, preferred_element_type=jnp...  19.7 us
    unnamed x138, local copies, waits for them, and re-layouts  15.4 us
    dot_general x1, matrix products, attend_back(): jnp.einsum('qhd,khd->hqk', queries, keys, preferred_element_type=jnp.floa...  13.3 us
    dot_general x1, matrix products, attend_back(): jnp.einsum('hqk,qhd->khd', probs.astype(jnp.bfloat16), grad_mixed, prefer...  13.2 us
  transfers between devices with their start and end apart: 16, of which 11 were waited for; matrix products, arithmetic and copies ran while one was open for 43% of the time, Pallas kernels for 0%

commit v1 on v0

--- a/solution.py
+++ b/solution.py
@@ -232,9 +232,10 @@
     grad_ada = jnp.einsum(
         "lc,lm->cm", cond_half.astype(jnp.float32), grad_modulation, precision=highest
     )
-    grad_cond = lax.psum(
-        jnp.einsum("lm,cm->lc", grad_modulation, w_ada.astype(jnp.float32), precision=highest), "dp"
-    ) * silu_slope(cond)
+    grad_cond = jax.lax.all_gather(
+        jnp.einsum("lm,cm->lc", grad_modulation, w_ada.astype(jnp.float32), precision=highest),
+        axis_name="dp",
+    ).sum(axis=0) * silu_slope(cond)
     grad_table = jnp.einsum("ln,lc->nc", one_hot.astype(jnp.float32), grad_cond, precision=highest)
     return (
         block_out[None],

time: 534 us -> 497 us (0.931)
  blocking collectives: 83.1 us -> 46.6 us
    psum x1 -> x0, blocking collectives: 59.8 us -> none  [shards(): lax.psum(jnp.einsum('lm,cm->lc', grad_modulation, w_ada.astype(jnp.float3...]
    all_gather x0 -> x1, blocking collectives: none -> 23.3 us  [shards(): jax.lax.all_gather(jnp.einsum('lm,cm->lc', grad_modulation, w_ada.astype(...]
    unnamed x138 -> x142, local copies, waits for them, and re-layouts: 15.4 us -> 15.4 us
  transfers between devices with their start and end apart: 16 -> 16, of which waited for: 11 -> 11; matrix products, arithmetic and copies ran while one was open for 43% -> 46% of each run, Pallas kernels for 0% -> 0%
where the time goes in v1:
time: 497 us; the launch traced here: 489 us
  matrix products  198 us (40%)
  waiting for transfers between devices  137 us (28%)
  blocking collectives  46.6 us (9%)
  other arithmetic  41.1 us (8%)
  local copies, waits for them, and re-layouts  27.7 us (6%)
  starting transfers between devices  22.9 us (5%)
  between operations  16.3 us (3%)
    ppermute x10, waiting for transfers between devices, from_rank(): lax.ppermute(value, 'tensor', [(i, (i - step) % ranks) for i in range(ran...  127 us
    dot_general x20, matrix products, dot(): return jnp.einsum(spec, left, right, preferred_element_type=jnp.float32)  110 us
    all_gather x1, blocking collectives, shards(): jax.lax.all_gather(jnp.einsum('lm,cm->lc', grad_modulation, w_ada.astype(...  23.3 us
    all_gather x1, blocking collectives, shards(): lax.all_gather(jnp.stack([steps, labels], axis=1), 'dp', axis=0, tiled=True)  23.3 us
    dot_general x1, matrix products, attend_back(): jnp.einsum('qhd,khd->hqk', grad_mixed, values, preferred_element_type=jnp...  19.7 us
    unnamed x142, local copies, waits for them, and re-layouts  15.4 us
    dot_general x1, matrix products, attend_back(): jnp.einsum('qhd,khd->hqk', queries, keys, preferred_element_type=jnp.floa...  13.3 us
    dot_general x1, matrix products, attend_back(): jnp.einsum('hqk,qhd->khd', probs.astype(jnp.bfloat16), grad_mixed, prefer...  13.2 us
  transfers between devices with their start and end apart: 16, of which 11 were waited for; matrix products, arithmetic and copies ran while one was open for 46% of the time, Pallas kernels for 0%

profile of v1, /device:TPU:0, one launch (start us, length us, event | category | flops | bytes accessed | tf_op | source)
XLA Modules:
  0.0 489.2 jit_solution(12180305109341438883)
XLA Ops:
  13.7 23.3 %all-gather.1 = s32[16,1,2]{2,1,0:T(1,128)S(1)} all-gather(s32[1,1,2]{2,1,0:T(1,128)S(1)} %add_bitcast_fusion.1), channel_id=1, replica_groups=mesh['dp'=16,'tensor'=2] {'dp'}, dimensions={0}, use_global_device_ids=true | all-gather | bytes 136 | tf_op jit(solution)/shard_map/all_gather | solution.py:133
  46.3 7.2 %all-to-all-done = f32[16,1,432]{2,1,0:T(1,128)S(1)} async-done(((f32[16,1,432]{2,1,0:T(1,128)}), f32[16,1,432]{2,1,0:T(1,128)S(1)}, u32[]{:S(2)}, u32[]{:S(2)}) %all-to-all-start) | async-done | bytes 27680 | tf_op jit(solution)/shard_map/all_to_all | solution.py:149
  56.5 25.9 %collective-permute-done.1 = bf16[512,1152]{1,0:T(8,128)(2,1)S(1)} collective-permute-done((bf16[512,1152]{1,0:T(8,128)(2,1)S(1)}, bf16[512,1152]{1,0:T(8,128)(2,1)S(1)}, u32[]{:S(2)}, u32[]{:S(2)}) %collective-permute-start.1) | collective-permute-done | bytes 1179680 | tf_op jit(solution)/shard_map/ppermute | solution.py:88
  118.3 14.8 %collective-permute-done.2 = bf16[512,1152]{1,0:T(8,128)(2,1)S(1)} collective-permute-done((bf16[512,1152]{1,0:T(8,128)(2,1)S(1)}, bf16[512,1152]{1,0:T(8,128)(2,1)S(1)}, u32[]{:S(2)}, u32[]{:S(2)}) %collective-permute-start.2) | collective-permute-done | bytes 1179680 | tf_op jit(solution)/shard_map/ppermute | solution.py:88
  142.5 25.7 %collective-permute-done.3 = bf16[512,1152]{1,0:T(8,128)(2,1)} collective-permute-done((bf16[512,1152]{1,0:T(8,128)(2,1)S(1)}, bf16[512,1152]{1,0:T(8,128)(2,1)}, u32[]{:S(2)}, u32[]{:S(2)}) %collective-permute-start.3) | collective-permute-done | bytes 1179680 | tf_op jit(solution)/shard_map/ppermute | solution.py:88
  168.2 8.4 %multiply_convert_fusion.1 = (bf16[512,2304]{1,0:T(8,128)(2,1)}, f32[512,2304]{1,0:T(8,128)S(1)}) fusion(bf16[512,1152]{1,0:T(8,128)(2,1)} %collective-permute-done.3, bf16[1152,4608]{1,0:T(8,128)(2,1)} %all-gather.7.cloned.1.call-done), kind=kOutput, calls=%fused_computation.39 | convolution fusion | flops 2728525824 | bytes 13565952 | tf_op jit(solution)/shard_map/td,df->tf/dot_general | solution.py:114
  176.5 13.8 %collective-permute-done.5 = bf16[512,1152]{1,0:T(8,128)(2,1)} collective-permute-done((bf16[512,1152]{1,0:T(8,128)(2,1)}, bf16[512,1152]{1,0:T(8,128)(2,1)}, u32[]{:S(2)}, u32[]{:S(2)}) %collective-permute-start.5) | collective-permute-done | bytes 1179680 | tf_op jit(solution)/shard_map/ppermute | solution.py:88
  206.6 7.4 %fusion.21 = bf16[512,2304]{1,0:T(8,128)(2,1)S(1)} fusion(f32[512,2304]{1,0:T(8,128)S(1)} %get-tuple-element.74, bf16[512,1152]{1,0:T(8,128)(2,1)} %fusion.65, bf16[1152,4608]{1,0:T(8,128)(2,1)S(1)} %copy-done.58), kind=kOutput, calls=%fused_computation.41 | convolution fusion | flops 2740322304 | bytes 13565952 | tf_op jit(solution)/shard_map/td,df->tf/dot_general | solution.py:114
  214.0 9.1 %convolution_convert_fusion.1 = bf16[1152,2304]{1,0:T(8,128)(2,1)S(1)} fusion(bf16[512,2304]{1,0:T(8,128)(2,1)} %copy-done.64, bf16[512,2304]{1,0:T(8,128)(2,1)S(1)} %fusion.21, bf16[512,1152]{1,0:T(8,128)(2,1)} %collective-permute-done.3, bf16[512,1152]{1,0:T(8,128)(2,1)S(1)} %copy-done.28), kind=kOutput, calls=%fused_computation.11 | convolution fusion | flops 5452627968 | bytes 12386304 | tf_op jit(solution)/shard_map/td,tf->df/dot_general | solution.py:114
  223.2 7.9 %convolution_convert_fusion = bf16[1152,2304]{1,0:T(8,128)(2,1)S(1)} fusion(bf16[512,2304]{1,0:T(8,128)(2,1)S(1)} %copy-done.63, bf16[512,2304]{1,0:T(8,128)(2,1)S(1)} %get-tuple-element.73, bf16[512,1152]{1,0:T(8,128)(2,1)} %collective-permute-done.5, bf16[512,1152]{1,0:T(8,128)(2,1)} %fusion.65), kind=kOutput, calls=%fused_computation.10 | convolution fusion | flops 5452627968 | bytes 12386304 | tf_op jit(solution)/shard_map/td,tf->df/dot_general | solution.py:114
  235.7 8.2 %convert_add_fusion.2 = f32[512,1152]{1,0:T(8,128)} fusion(bf16[512,1152]{1,0:T(8,128)(2,1)} %collective-permute-done.6, bf16[512,2304]{1,0:T(8,128)(2,1)} %copy-done.60, bf16[1152,4608]{1,0:T(8,128)(2,1)} %all-gather.7.cloned.1.call-done), kind=kOutput, calls=%fused_computation.116 | convolution fusion | flops 2719088640 | bytes 11206656 | tf_op jit(solution)/shard_map/tf,df->td/dot_general | solution.py:114
  251.8 6.8 %fusion.27 = f32[512,1152]{1,0:T(8,128)S(1)} fusion(bf16[512,2304]{1,0:T(8,128)(2,1)S(1)} %copy-done.62, bf16[1152,4608]{1,0:T(8,128)(2,1)} %all-gather.7.cloned.1.call-done), kind=kOutput, calls=%fused_computation.55 | convolution fusion | flops 2717908992 | bytes 10027008 | tf_op jit(solution)/shard_map/tf,df->td/dot_general | solution.py:114
  260.4 15.6 %collective-permute-done.4 = bf16[512,1152]{1,0:T(8,128)(2,1)S(1)} collective-permute-done((bf16[512,1152]{1,0:T(8,128)(2,1)S(1)}, bf16[512,1152]{1,0:T(8,128)(2,1)S(1)}, u32[]{:S(2)}, u32[]{:S(2)}) %collective-permute-start.4) | collective-permute-done | bytes 1179680 | tf_op jit(solution)/shard_map/ppermute | solution.py:88
  282.2 13.3 %fusion.134 = f32[8,1024,1024]{2,1,0:T(8,128)} fusion(bf16[1024,8,72]{0,2,1:T(8,128)(2,1)S(1)} %bitcast.146, bf16[1024,8,72]{0,2,1:T(8,128)(2,1)S(1)} %bitcast.141), kind=kOutput, calls=%fused_computation.218 | convolution fusion | flops 1207959552 | bytes 35913728 | tf_op jit(solution)/shard_map/qhd,khd->hqk/dot_general | solution.py:71
  297.1 8.4 %collective-permute-done.7 = bf16[512,1152]{1,0:T(8,128)(2,1)S(1)} collective-permute-done((bf16[512,1152]{1,0:T(8,128)(2,1)S(1)}, bf16[512,1152]{1,0:T(8,128)(2,1)S(1)}, u32[]{:S(2)}, u32[]{:S(2)}) %collective-permute-start.7) | collective-permute-done | bytes 1179680 | tf_op jit(solution)/shard_map/ppermute | solution.py:88
  310.4 19.7 %multiply_convert_fusion = bf16[8,1024,1024]{2,1,0:T(8,128)(2,1)} fusion(f32[8,1024,1024]{2,1,0:T(8,128)} %fusion.134, f32[8,1024]{1,0:T(8,128)S(1)} %bitcast.172, f32[8,1024]{1,0:T(8,128)S(1)} %pad_maximum_fusion.7, bf16[1024,8,72]{0,2,1:T(8,128)(2,1)S(1)} %bitcast.144, bf16[1024,8,72]{0,2,1:T(8,128)(2,1)S(1)} %bitcast.150), kind=kOutput, calls=%fused_computation | convolution fusion | flops 1258291200 | bytes 52756480 | tf_op jit(solution)/shard_map/qhd,khd->hqk/dot_general | solution.py:77
  330.1 9.1 %convolution_convert_fusion.8 = bf16[8,72,1024]{2,1,0:T(8,128)(2,1)S(1)} fusion(bf16[1024,8,72]{0,2,1:T(8,128)(2,1)S(1)} %bitcast.147, bf16[8,1024,1024]{2,1,0:T(8,128)(2,1)} %multiply_convert_fusion), kind=kOutput, calls=%fused_computation.128 | convolution fusion | flops 1208549376 | bytes 19136512 | tf_op jit(solution)/shard_map/hqk,qhd->khd/dot_general | solution.py:83
  339.2 12.1 %convolution_convert_fusion.9 = bf16[8,72,1024]{2,1,0:T(8,128)(2,1)} fusion(bf16[1024,8,72]{0,2,1:T(8,128)(2,1)S(1)} %bitcast.142, bf16[8,1024,1024]{2,1,0:T(8,128)(2,1)} %multiply_convert_fusion), kind=kOutput, calls=%fused_computation.129 | convolution fusion | flops 1208549376 | bytes 19136512 | tf_op jit(solution)/shard_map/hqk,khd->qhd/dot_general | solution.py:82
  351.2 13.2 %fusion.85 = bf16[8,72,1024]{2,1,0:T(8,128)(2,1)S(1)} fusion(bf16[1024,8,72]{0,2,1:T(8,128)(2,1)S(1)} %bitcast.145, f32[8,1024,1024]{2,1,0:T(8,128)} %fusion.134, f32[8,1024]{1,0:T(8,128)} %copy-done.29), kind=kOutput, calls=%fused_computation.127 | convolution fusion | flops 1233715200 | bytes 35946496 | tf_op jit(solution)/shard_map/hqk,qhd->khd/dot_general | solution.py:74
  364.5 9.1 %convolution_convert_fusion.2 = bf16[1152,1728]{0,1:T(8,128)(2,1)S(1)} fusion(bf16[512,1152]{1,0:T(8,128)(2,1)} %copy-done.59, bf16[512,1152]{1,0:T(8,128)(2,1)} %copy-done.26, bf16[1024,576]{0,1:T(8,128)(2,1)S(1)} %bitcast.151, bf16[1024,576]{0,1:T(8,128)(2,1)S(1)} %bitcast.156, bf16[1024,576]{0,1:T(8,128)(2,1)S(1)} %bitcast.158), kind=kOutput, calls=%fused_computation.15 | convolution fusion | flops 4094189568 | bytes 9879552 | tf_op jit(solution)/shard_map/td,tc->dc/dot_general | solution.py:114
  378.7 8.6 %copy.25 = bf16[1152,2304]{1,0:T(8,128)(2,1)} copy(bf16[1152,2304]{0,1:T(8,128)(2,1)} %pad_maximum_fusion.1) | data formatting | bytes 10616832
  397.9 19.9 %collective-permute-done.8 = bf16[512,1152]{1,0:T(8,128)(2,1)S(1)} collective-permute-done((bf16[512,1152]{1,0:T(8,128)(2,1)S(1)}, bf16[512,1152]{1,0:T(8,128)(2,1)S(1)}, u32[]{:S(2)}, u32[]{:S(2)}) %collective-permute-start.8) | collective-permute-done | bytes 1179680 | tf_op jit(solution)/shard_map/ppermute | solution.py:88
  432.8 8.6 %all-to-all-start.1 = ((f32[16,1,432]{2,1,0:T(1,128)}), f32[16,1,432]{2,1,0:T(1,128)}, u32[]{:S(2)}, u32[]{:S(2)}) async-start(f32[16,1,432]{2,1,0:T(1,128)} %all_to_all.16), calls=%async_computation.1 | async-start | bytes 65536 | tf_op jit(solution)/shard_map/all_to_all | solution.py:231
  449.5 23.3 %all-gather = f32[256,576]{1,0:T(8,128)S(1)} all-gather(f32[16,576]{1,0:T(8,128)S(1)} %fusion.110), channel_id=2, replica_groups=mesh['dp'=16,'tensor'=2] {'dp'}, dimensions={0}, use_global_device_ids=true | all-gather | bytes 626688 | tf_op jit(solution)/shard_map/all_gather | solution.py:235
  (252 shorter events, 153.8 us)
Async XLA Ops:
  7.2 75.1 %all-gather.5.cloned.1.call-start = ((), (), s32[]{:S(2)}) async-start(), calls=%async_computation.4 | async-start | bytes 5640192 | tf_op jit(solution)/shard_map/all_gather | solution.py:135
  8.4 31.3 %copy-start.2 = (bf16[1,512,1152]{2,1,0:T(8,128)(2,1)S(1)}, bf16[1,512,1152]{2,1,0:T(8,128)(2,1)}, u32[]{:S(2)}) copy-start(bf16[1,512,1152]{2,1,0:T(8,128)(2,1)} %param.10) | copy-start | bytes 3538948
  10.3 157.8 %all-gather.7.cloned.1.call-start = ((), (), s32[]{:S(2)}) async-start(), calls=%async_computation.5 | async-start | bytes 11280384 | tf_op jit(solution)/shard_map/all_gather | solution.py:138
  38.2 3.9 collective-permute-start
  39.9 47.6 %copy-start.50 = (f32[512]{0:T(512)}, f32[512]{0:T(512)S(1)}, u32[]{:S(2)}) copy-start(f32[512]{0:T(512)S(1)} %broadcast_multiply_fusion.5) | copy-start | bytes 6148
  42.8 10.7 %all-to-all-start = ((f32[16,1,432]{2,1,0:T(1,128)}), f32[16,1,432]{2,1,0:T(1,128)S(1)}, u32[]{:S(2)}, u32[]{:S(2)}) async-start(f32[16,1,432]{2,1,0:T(1,128)} %copy.22), calls=%async_computation | async-start | bytes 65536 | tf_op jit(solution)/shard_map/all_to_all | solution.py:149
  46.3 330.2 %reduce-scatter.5.cloned.1.call-start = ((), (), s32[]{:S(2)}) async-start(), calls=%async_computation.6 | async-start | bytes 11280384 | tf_op jit(solution)/shard_map/reduce_scatter | solution.py:193
  46.3 41.2 %copy-start.53 = (f32[512]{0:T(512)}, f32[512]{0:T(512)S(1)}, u32[]{:S(2)}) copy-start(f32[512]{0:T(512)S(1)} %add_rsqrt_fusion.1) | copy-start | bytes 6148
  55.0 32.6 %copy-start.26 = (bf16[512,1152]{1,0:T(8,128)(2,1)}, bf16[512,1152]{1,0:T(8,128)(2,1)S(1)}, u32[]{:S(2)}) copy-start(bf16[512,1152]{1,0:T(8,128)(2,1)S(1)} %fusion.57) | copy-start | bytes 3538948
  55.0 27.4 %collective-permute-start.1 = (bf16[512,1152]{1,0:T(8,128)(2,1)S(1)}, bf16[512,1152]{1,0:T(8,128)(2,1)S(1)}, u32[]{:S(2)}, u32[]{:S(2)}) collective-permute-start(bf16[512,1152]{1,0:T(8,128)(2,1)S(1)} %fusion.57), channel_id=1, source_target_pairs={{0,1},{1,0},{2,3},{3,2},{4,5},{5,4},{6,7},{7,6},{8,9},{9,8},{10,11... | collective-permute-start | bytes 3538952 | tf_op jit(solution)/shard_map/ppermute | solution.py:88
  106.4 26.6 %collective-permute-start.2 = (bf16[512,1152]{1,0:T(8,128)(2,1)S(1)}, bf16[512,1152]{1,0:T(8,128)(2,1)S(1)}, u32[]{:S(2)}, u32[]{:S(2)}) collective-permute-start(bf16[512,1152]{1,0:T(8,128)(2,1)S(1)} %convolution_convert_fusion.5), channel_id=1, source_target_pairs={{0,1},{1,0},{2,3},{3,2},{4,5},{5,4},{6,7},{7,6},{8,9},{9,8},{10,11... | collective-permute-start | bytes 3538952 | tf_op jit(solution)/shard_map/ppermute | solution.py:88
  139.1 29.0 %collective-permute-start.3 = (bf16[512,1152]{1,0:T(8,128)(2,1)S(1)}, bf16[512,1152]{1,0:T(8,128)(2,1)}, u32[]{:S(2)}, u32[]{:S(2)}) collective-permute-start(bf16[512,1152]{1,0:T(8,128)(2,1)S(1)} %add_convert_fusion.1), channel_id=1, source_target_pairs={{0,1},{1,0},{2,3},{3,2},{4,5},{5,4},{6,7},{7,6},{8,9},{9,8},{10,11... | collective-permute-start | bytes 3538952 | tf_op jit(solution)/shard_map/ppermute | solution.py:88
  141.9 48.4 %collective-permute-start.5 = (bf16[512,1152]{1,0:T(8,128)(2,1)}, bf16[512,1152]{1,0:T(8,128)(2,1)}, u32[]{:S(2)}, u32[]{:S(2)}) collective-permute-start(bf16[512,1152]{1,0:T(8,128)(2,1)} %fusion.65), channel_id=1, source_target_pairs={{0,1},{1,0},{2,3},{3,2},{4,5},{5,4},{6,7},{7,6},{8,9},{9,8},{10,11... | collective-permute-start | bytes 3538952 | tf_op jit(solution)/shard_map/ppermute | solution.py:88
  201.2 34.5 %collective-permute-start.6 = (bf16[512,1152]{1,0:T(8,128)(2,1)}, bf16[512,1152]{1,0:T(8,128)(2,1)}, u32[]{:S(2)}, u32[]{:S(2)}) collective-permute-start(bf16[512,1152]{1,0:T(8,128)(2,1)} %fusion.37), channel_id=1, source_target_pairs={{0,1},{1,0},{2,3},{3,2},{4,5},{5,4},{6,7},{7,6},{8,9},{9,8},{10,11... | collective-permute-start | bytes 3538952 | tf_op jit(solution)/shard_map/ppermute | solution.py:88
  243.8 235.1 %reduce-scatter.7.cloned.1.call-start = ((), (), s32[]{:S(2)}) async-start(), calls=%async_computation.7 | async-start | bytes 5640192
  244.6 65.8 %copy-start.29 = (f32[8,1024]{1,0:T(8,128)}, f32[8,1024]{1,0:T(8,128)S(1)}, u32[]{:S(2)}) copy-start(f32[8,1024]{1,0:T(8,128)S(1)} %pad_maximum_fusion.7) | copy-start | bytes 98308
  251.3 24.7 %collective-permute-start.4 = (bf16[512,1152]{1,0:T(8,128)(2,1)S(1)}, bf16[512,1152]{1,0:T(8,128)(2,1)S(1)}, u32[]{:S(2)}, u32[]{:S(2)}) collective-permute-start(bf16[512,1152]{1,0:T(8,128)(2,1)S(1)} %fusion.40), channel_id=1, source_target_pairs={{0,1},{1,0},{2,3},{3,2},{4,5},{5,4},{6,7},{7,6},{8,9},{9,8},{10,11... | collective-permute-start | bytes 3538952 | tf_op jit(solution)/shard_map/ppermute | solution.py:88
  281.6 23.8 %collective-permute-start.7 = (bf16[512,1152]{1,0:T(8,128)(2,1)S(1)}, bf16[512,1152]{1,0:T(8,128)(2,1)S(1)}, u32[]{:S(2)}, u32[]{:S(2)}) collective-permute-start(bf16[512,1152]{1,0:T(8,128)(2,1)S(1)} %multiply_convert_fusion.3), channel_id=1, source_target_pairs={{0,1},{1,0},{2,3},{3,2},{4,5},{5,4},{6,7},{7,6},{8,9},{9,8},{10,11... | collective-permute-start | bytes 3538952 | tf_op jit(solution)/shard_map/ppermute | solution.py:88
  394.4 23.4 %collective-permute-start.8 = (bf16[512,1152]{1,0:T(8,128)(2,1)S(1)}, bf16[512,1152]{1,0:T(8,128)(2,1)S(1)}, u32[]{:S(2)}, u32[]{:S(2)}) collective-permute-start(bf16[512,1152]{1,0:T(8,128)(2,1)S(1)} %convolution_convert_fusion.4), channel_id=1, source_target_pairs={{0,1},{1,0},{2,3},{3,2},{4,5},{5,4},{6,7},{7,6},{8,9},{9,8},{10,11... | collective-permute-start | bytes 3538952 | tf_op jit(solution)/shard_map/ppermute | solution.py:88
  397.9 43.5 %copy-start.6 = (f32[512,1152]{1,0:T(8,128)S(1)}, f32[512,1152]{1,0:T(8,128)}, u32[]{:S(2)}) copy-start(f32[512,1152]{1,0:T(8,128)} %copy-done.5) | copy-start | bytes 7077892
  397.9 43.5 %copy-start.52 = (f32[512]{0:T(512)S(1)}, f32[512]{0:T(512)}, u32[]{:S(2)}) copy-start(f32[512]{0:T(512)} %copy-done.50) | copy-start | bytes 6148
  397.9 43.5 %copy-start.55 = (f32[512]{0:T(512)S(1)}, f32[512]{0:T(512)}, u32[]{:S(2)}) copy-start(f32[512]{0:T(512)} %copy-done.53) | copy-start | bytes 6148
  427.2 4.1 collective-permute-start.9
  432.8 15.3 %all-to-all-start.1 = ((f32[16,1,432]{2,1,0:T(1,128)}), f32[16,1,432]{2,1,0:T(1,128)}, u32[]{:S(2)}, u32[]{:S(2)}) async-start(f32[16,1,432]{2,1,0:T(1,128)} %all_to_all.16), calls=%async_computation.1 | async-start | bytes 65536 | tf_op jit(solution)/shard_map/all_to_all | solution.py:231
  (62 other events, 735.0 us)
Sparse Core Ops, SparseCore 0:
  10.7 59.4 all-gather.4
  73.0 86.9 all-gather.6
  244.0 120.1 reduce-scatter.4
  387.4 82.3 reduce-scatter.6
